TPU v7x, 32 devices: a whole 2x2x4 slice. The times are simulated.
32 devices in a mesh: outer: 4 (over y, core), inner: 8 (over z, x).
Axes of the slice: x: 2, y: 2, z: 4, core: 2. Of those that a mesh axis runs over, the one named last changes fastest.
Arguments:
- queries: bfloat16 [4096, 2048], P(('outer', 'inner')), may hold values from -2 to 2
- keys: bfloat16 [4096, 2048], P(('outer', 'inner')), may hold values from -2 to 2
- values: bfloat16 [4096, 2048], P(('outer', 'inner')), may hold values from -6 to 6
- grad_out: bfloat16 [4096, 2048], P(('outer', 'inner')), may hold values from -96 to 96
- window: int32 [1], replicated, may hold values from 513 to 640
Outputs:
- query_grad: bfloat16 [4096, 2048], P(('outer', 'inner'))
- key_grad: bfloat16 [4096, 2048], P(('outer', 'inner'))
- value_grad: bfloat16 [4096, 2048], P(('outer', 'inner'))
All inputs are finite; a program needn't handle non-finite values.
Results may differ from a plain program's by a relative error of at most 0.0085.
Values may be sent and summed in bfloat16 or wider, within the bound.
A program may use at most 64 MiB of HBM per device.

v0:
```python
import jax
import jax.numpy as jnp
from jax import lax
from jax.sharding import PartitionSpec as P

HEADS = 16
HD = 128


def shifted(value, axis, steps):
    count = lax.axis_size(axis)
    first, last = (max(0, -steps), min(count, count - steps))
    return lax.ppermute(value, axis, [(source, source + steps) for source in range(first, last)])


def visible(query_start, key_start, count, width, total):
    query_pos = query_start + jnp.arange(count, dtype=jnp.int32)[:, None]
    key_pos = key_start + jnp.arange(count, dtype=jnp.int32)[None, :]
    return (
        (key_pos <= query_pos)
        & (key_pos > query_pos - width)
        & (key_pos >= 0)
        & (query_pos < total)
    )


def head_scores(query_block, key_block):
    return jnp.einsum(
        "qhd,khd->hqk", query_block, key_block, preferred_element_type=jnp.float32
    ) * HD ** (-0.5)


def pair_grads(query_block, out_grad, log_norm, centre, key_block, value_block, allowed):
    scale = HD ** (-0.5)
    logits = head_scores(query_block, key_block)
    probs = jnp.where(allowed[None], jnp.exp(logits - log_norm[:, :, None]), 0.0)
    probs_low = probs.astype(jnp.bfloat16)
    value_term = jnp.einsum("hqk,qhd->khd", probs_low, out_grad, preferred_element_type=jnp.float32)
    prob_grad = jnp.einsum(
        "qhd,khd->hqk", out_grad, value_block, preferred_element_type=jnp.float32
    )
    logit_grad = (probs * (prob_grad - centre[:, :, None])).astype(jnp.bfloat16)
    query_term = (
        jnp.einsum("hqk,khd->qhd", logit_grad, key_block, preferred_element_type=jnp.float32)
        * scale
    )
    key_term = (
        jnp.einsum("hqk,qhd->khd", logit_grad, query_block, preferred_element_type=jnp.float32)
        * scale
    )
    return (
        query_term.astype(jnp.bfloat16),
        key_term.astype(jnp.bfloat16),
        value_term.astype(jnp.bfloat16),
    )


def per_device(queries, keys, values, grad_out, window):
    count = queries.shape[0]
    total = lax.axis_size(("outer", "inner")) * count
    start = lax.axis_index(("outer", "inner")) * count
    width = window[0]
    shaped = (count, HEADS, HD)
    query_block = queries.reshape(shaped)
    key_block = keys.reshape(shaped)
    value_block = values.reshape(shaped)
    grad_block = grad_out.reshape(shaped)
    fetched = [(key_block, value_block)]
    passing = (key_block, value_block)
    for hop in range(1, 6):
        passing = shifted((passing[0], passing[1]), ("outer", "inner"), 1)
        fetched.append(passing)
    norm_total = jnp.zeros((HEADS, count), jnp.float32)
    weighted = jnp.zeros(shaped, jnp.float32)
    for hop in range(6):
        allowed = visible(start, start - hop * count, count, width, total)
        logits = head_scores(query_block, fetched[hop][0])
        weights = jnp.where(allowed[None], jnp.exp(logits), 0.0)
        norm_total = norm_total + jnp.sum(weights, axis=2)
        weighted = weighted + jnp.einsum(
            "hqk,khd->qhd",
            weights.astype(jnp.bfloat16),
            fetched[hop][1],
            preferred_element_type=jnp.float32,
        )
    log_norm = jnp.log(norm_total)
    output = weighted / jnp.transpose(norm_total)[:, :, None]
    centre = jnp.transpose(jnp.sum(grad_block.astype(jnp.float32) * output, axis=2))
    query_total = jnp.zeros(shaped, jnp.float32)
    key_total = jnp.zeros(shaped, jnp.float32)
    value_total = jnp.zeros(shaped, jnp.float32)
    for hop in range(6):
        allowed = visible(start, start - hop * count, count, width, total)
        query_term, key_term, value_term = pair_grads(
            query_block, grad_block, log_norm, centre, fetched[hop][0], fetched[hop][1], allowed
        )
        query_total = query_total + query_term.astype(jnp.float32)
        if hop == 0:
            key_total = key_term.astype(jnp.float32)
            value_total = value_term.astype(jnp.float32)
        else:
            returned = shifted((key_term, value_term), ("outer", "inner"), -hop)
            key_total = key_total + returned[0].astype(jnp.float32)
            value_total = value_total + returned[1].astype(jnp.float32)
    flat = (count, HEADS * HD)
    return (
        query_total.reshape(flat).astype(jnp.bfloat16),
        key_total.reshape(flat).astype(jnp.bfloat16),
        value_total.reshape(flat).astype(jnp.bfloat16),
    )


def solution(mesh):
    placed = (
        P(("outer", "inner"), None),
        P(("outer", "inner"), None),
        P(("outer", "inner"), None),
        P(("outer", "inner"), None),
        P(),
    )
    return jax.shard_map(
        per_device,
        mesh=mesh,
        in_specs=placed,
        out_specs=(
            P(("outer", "inner"), None),
            P(("outer", "inner"), None),
            P(("outer", "inner"), None),
        ),
        check_vma=False,
    )
```

profile of v0, /device:TPU:27, one launch (start us, length us, event | category | flops | bytes accessed | tf_op | source)
XLA Modules:
  0.0 300.5 jit_solution(17085013675418819730)
XLA Ops:
  0.7 1.4 copy.88
  2.1 3.3 %collective-permute-start.5 = (bf16[128,16,128]{0,2,1:T(8,128)(2,1)S(1)}, bf16[128,16,128]{0,2,1:T(8,128)(2,1)}, u32[]{:S(2)}, u32[]{:S(2)}) collective-permute-start(bf16[128,16,128]{0,2,1:T(8,128)(2,1)S(1)} %bitcast.185), channel_id=1, source_target_pairs={{0,1},{1,2},{2,3},{3,4},{4,5},{5,6},{6,7},{7,8},{8,9},{9,10},{10,1... | collective-permute-start | bytes 1572872 | tf_op jit(solution)/shard_map/ppermute | solution.py:13
  5.7 1.0 copy.81
  6.7 3.4 %collective-permute-start = (bf16[128,16,128]{2,0,1:T(8,128)(2,1)}, bf16[128,16,128]{2,0,1:T(8,128)(2,1)}, u32[]{:S(2)}, u32[]{:S(2)}) collective-permute-start(bf16[128,16,128]{2,0,1:T(8,128)(2,1)} %copy.81), channel_id=1, source_target_pairs={{0,1},{1,2},{2,3},{3,4},{4,5},{5,6},{6,7},{7,8},{8,9},{9,10},{10,1... | collective-permute-start | bytes 1572872 | tf_op jit(solution)/shard_map/ppermute | solution.py:13
  11.5 0.5 fusion.55
  12.3 4.8 %collective-permute-done.5 = bf16[128,16,128]{0,2,1:T(8,128)(2,1)} collective-permute-done((bf16[128,16,128]{0,2,1:T(8,128)(2,1)S(1)}, bf16[128,16,128]{0,2,1:T(8,128)(2,1)}, u32[]{:S(2)}, u32[]{:S(2)}) %collective-permute-start.5) | collective-permute-done | bytes 524320 | tf_op jit(solution)/shard_map/ppermute | solution.py:13
  17.1 8.1 %collective-permute-start.6 = (bf16[128,16,128]{0,2,1:T(8,128)(2,1)}, bf16[128,16,128]{0,2,1:T(8,128)(2,1)S(1)}, u32[]{:S(2)}, u32[]{:S(2)}) collective-permute-start(bf16[128,16,128]{0,2,1:T(8,128)(2,1)} %collective-permute-done.5), channel_id=1, source_target_pairs={{0,1},{1,2},{2,3},{3,4},{4,5},{5,6},{6,7},{7,8},{8,9},{9,10},{10,1... | collective-permute-start | bytes 1572872 | tf_op jit(solution)/shard_map/ppermute | solution.py:13
  25.2 3.3 %collective-permute-done = bf16[128,16,128]{2,0,1:T(8,128)(2,1)} collective-permute-done((bf16[128,16,128]{2,0,1:T(8,128)(2,1)}, bf16[128,16,128]{2,0,1:T(8,128)(2,1)}, u32[]{:S(2)}, u32[]{:S(2)}) %collective-permute-start) | collective-permute-done | bytes 524320 | tf_op jit(solution)/shard_map/ppermute | solution.py:13
  28.5 8.0 %collective-permute-start.1 = (bf16[128,16,128]{2,0,1:T(8,128)(2,1)}, bf16[128,16,128]{2,0,1:T(8,128)(2,1)S(1)}, u32[]{:S(2)}, u32[]{:S(2)}) collective-permute-start(bf16[128,16,128]{2,0,1:T(8,128)(2,1)} %collective-permute-done), channel_id=1, source_target_pairs={{0,1},{1,2},{2,3},{3,4},{4,5},{5,6},{6,7},{7,8},{8,9},{9,10},{10,1... | collective-permute-start | bytes 1572872 | tf_op jit(solution)/shard_map/ppermute | solution.py:13
  36.4 1.6 fusion.57
  38.0 1.4 convolution_add_fusion.4
  39.7 7.9 %collective-permute-start.7 = (bf16[128,16,128]{0,2,1:T(8,128)(2,1)S(1)}, bf16[128,16,128]{0,2,1:T(8,128)(2,1)S(1)}, u32[]{:S(2)}, u32[]{:S(2)}) collective-permute-start(bf16[128,16,128]{0,2,1:T(8,128)(2,1)S(1)} %collective-permute-done.6), channel_id=1, source_target_pairs={{0,1},{1,2},{2,3},{3,4},{4,5},{5,6},{6,7},{7,8},{8,9},{9,10},{10,1... | collective-permute-start | bytes 1572872 | tf_op jit(solution)/shard_map/ppermute | solution.py:13
  47.6 3.4 %collective-permute-done.1 = bf16[128,16,128]{2,0,1:T(8,128)(2,1)S(1)} collective-permute-done((bf16[128,16,128]{2,0,1:T(8,128)(2,1)}, bf16[128,16,128]{2,0,1:T(8,128)(2,1)S(1)}, u32[]{:S(2)}, u32[]{:S(2)}) %collective-permute-start.1) | collective-permute-done | bytes 524320 | tf_op jit(solution)/shard_map/ppermute | solution.py:13
  50.9 7.9 %collective-permute-start.2 = (bf16[128,16,128]{2,0,1:T(8,128)(2,1)S(1)}, bf16[128,16,128]{2,0,1:T(8,128)(2,1)S(1)}, u32[]{:S(2)}, u32[]{:S(2)}) collective-permute-start(bf16[128,16,128]{2,0,1:T(8,128)(2,1)S(1)} %collective-permute-done.1), channel_id=1, source_target_pairs={{0,1},{1,2},{2,3},{3,4},{4,5},{5,6},{6,7},{7,8},{8,9},{9,10},{10,1... | collective-permute-start | bytes 1572872 | tf_op jit(solution)/shard_map/ppermute | solution.py:13
  58.8 0.5 fusion.59
  59.6 2.4 collective-permute-done.7
  62.1 8.0 %collective-permute-start.8 = (bf16[128,16,128]{0,2,1:T(8,128)(2,1)S(1)}, bf16[128,16,128]{0,2,1:T(8,128)(2,1)S(1)}, u32[]{:S(2)}, u32[]{:S(2)}) collective-permute-start(bf16[128,16,128]{0,2,1:T(8,128)(2,1)S(1)} %collective-permute-done.7), channel_id=1, source_target_pairs={{0,1},{1,2},{2,3},{3,4},{4,5},{5,6},{6,7},{7,8},{8,9},{9,10},{10,1... | collective-permute-start | bytes 1572872 | tf_op jit(solution)/shard_map/ppermute | solution.py:13
  70.0 3.3 %collective-permute-done.2 = bf16[128,16,128]{2,0,1:T(8,128)(2,1)S(1)} collective-permute-done((bf16[128,16,128]{2,0,1:T(8,128)(2,1)S(1)}, bf16[128,16,128]{2,0,1:T(8,128)(2,1)S(1)}, u32[]{:S(2)}, u32[]{:S(2)}) %collective-permute-start.2) | collective-permute-done | bytes 524320 | tf_op jit(solution)/shard_map/ppermute | solution.py:13
  73.3 8.0 %collective-permute-start.3 = (bf16[128,16,128]{2,0,1:T(8,128)(2,1)S(1)}, bf16[128,16,128]{2,0,1:T(8,128)(2,1)S(1)}, u32[]{:S(2)}, u32[]{:S(2)}) collective-permute-start(bf16[128,16,128]{2,0,1:T(8,128)(2,1)S(1)} %collective-permute-done.2), channel_id=1, source_target_pairs={{0,1},{1,2},{2,3},{3,4},{4,5},{5,6},{6,7},{7,8},{8,9},{9,10},{10,1... | collective-permute-start | bytes 1572872 | tf_op jit(solution)/shard_map/ppermute | solution.py:13
  81.3 0.5 fusion.61
  82.1 2.4 collective-permute-done.8
  84.5 8.0 %collective-permute-start.9 = (bf16[128,16,128]{0,2,1:T(8,128)(2,1)S(1)}, bf16[128,16,128]{0,2,1:T(8,128)(2,1)S(1)}, u32[]{:S(2)}, u32[]{:S(2)}) collective-permute-start(bf16[128,16,128]{0,2,1:T(8,128)(2,1)S(1)} %collective-permute-done.8), channel_id=1, source_target_pairs={{0,1},{1,2},{2,3},{3,4},{4,5},{5,6},{6,7},{7,8},{8,9},{9,10},{10,1... | collective-permute-start | bytes 1572872 | tf_op jit(solution)/shard_map/ppermute | solution.py:13
  92.5 3.3 %collective-permute-done.3 = bf16[128,16,128]{2,0,1:T(8,128)(2,1)S(1)} collective-permute-done((bf16[128,16,128]{2,0,1:T(8,128)(2,1)S(1)}, bf16[128,16,128]{2,0,1:T(8,128)(2,1)S(1)}, u32[]{:S(2)}, u32[]{:S(2)}) %collective-permute-start.3) | collective-permute-done | bytes 524320 | tf_op jit(solution)/shard_map/ppermute | solution.py:13
  95.8 8.0 %collective-permute-start.4 = (bf16[128,16,128]{2,0,1:T(8,128)(2,1)S(1)}, bf16[128,16,128]{2,0,1:T(8,128)(2,1)S(1)}, u32[]{:S(2)}, u32[]{:S(2)}) collective-permute-start(bf16[128,16,128]{2,0,1:T(8,128)(2,1)S(1)} %collective-permute-done.3), channel_id=1, source_target_pairs={{0,1},{1,2},{2,3},{3,4},{4,5},{5,6},{6,7},{7,8},{8,9},{9,10},{10,1... | collective-permute-start | bytes 1572872 | tf_op jit(solution)/shard_map/ppermute | solution.py:13
  103.8 0.5 fusion.63
  104.6 13.3 %collective-permute-done.4 = bf16[128,16,128]{2,0,1:T(8,128)(2,1)S(1)} collective-permute-done((bf16[128,16,128]{2,0,1:T(8,128)(2,1)S(1)}, bf16[128,16,128]{2,0,1:T(8,128)(2,1)S(1)}, u32[]{:S(2)}, u32[]{:S(2)}) %collective-permute-start.4) | collective-permute-done | bytes 524320 | tf_op jit(solution)/shard_map/ppermute | solution.py:13
  117.9 0.5 fusion.65
  118.4 1.3 fusion.52
  119.7 1.3 fusion.51
  121.0 1.3 fusion.50
  122.3 1.3 fusion.53
  123.6 0.4 fusion.43
  124.0 0.4 fusion.9
  124.5 0.8 copy-done.1
  125.6 0.4 fusion.14
  126.0 0.5 fusion.44
  126.5 2.8 collective-permute-start.14
  129.4 0.4 fusion.13
  129.8 0.5 fusion.45
  130.3 5.6 %collective-permute-start.13 = (bf16[128,16,128]{0,2,1:T(8,128)(2,1)S(1)}, bf16[128,16,128]{0,2,1:T(8,128)(2,1)S(1)}, u32[]{:S(2)}, u32[]{:S(2)}) collective-permute-start(bf16[128,16,128]{0,2,1:T(8,128)(2,1)S(1)} %fusion.45), channel_id=1, source_target_pairs={{4,0},{5,1},{6,2},{7,3},{8,4},{9,5},{10,6},{11,7},{12,8},{13,9},{1... | collective-permute-start | bytes 1572872 | tf_op jit(solution)/shard_map/ppermute | solution.py:13
  136.0 0.4 fusion.12
  136.4 0.5 fusion.46
  136.9 2.1 collective-permute-start.12
  139.0 0.4 fusion.11
  139.5 0.5 fusion.47
  140.0 2.4 collective-permute-start.11
  142.4 1.5 fusion.10
  143.9 0.5 fusion.48
  144.4 2.9 collective-permute-start.10
  147.4 1.4 fusion.19
  149.5 1.3 fusion.49
  151.2 2.8 collective-permute-start.19
  154.0 70.2 %collective-permute-done.13 = bf16[128,16,128]{0,2,1:T(8,128)(2,1)S(1)} collective-permute-done((bf16[128,16,128]{0,2,1:T(8,128)(2,1)S(1)}, bf16[128,16,128]{0,2,1:T(8,128)(2,1)S(1)}, u32[]{:S(2)}, u32[]{:S(2)}) %collective-permute-start.13) | collective-permute-done | bytes 524320 | tf_op jit(solution)/shard_map/ppermute | solution.py:13
  224.1 1.9 collective-permute-start.18
  226.1 1.9 collective-permute-start.17
  228.0 1.9 collective-permute-start.16
  230.0 1.9 collective-permute-start.15
  232.3 1.0 copy.147
  233.4 2.3 add_convert_fusion.1
  235.7 1.0 copy.148
  236.7 32.1 %collective-permute-done.18 = bf16[128,16,128]{0,2,1:T(8,128)(2,1)} collective-permute-done((bf16[128,16,128]{0,2,1:T(8,128)(2,1)}, bf16[128,16,128]{0,2,1:T(8,128)(2,1)}, u32[]{:S(2)}, u32[]{:S(2)}) %collective-permute-start.18) | collective-permute-done | bytes 524320 | tf_op jit(solution)/shard_map/ppermute | solution.py:13
  268.8 28.3 %collective-permute-done.17 = bf16[128,16,128]{0,2,1:T(8,128)(2,1)} collective-permute-done((bf16[128,16,128]{0,2,1:T(8,128)(2,1)}, bf16[128,16,128]{0,2,1:T(8,128)(2,1)}, u32[]{:S(2)}, u32[]{:S(2)}) %collective-permute-start.17) | collective-permute-done | bytes 524320 | tf_op jit(solution)/shard_map/ppermute | solution.py:13
  297.1 2.3 add_convert_fusion
  299.5 1.0 copy.149
  (49 shorter events, 4.2 us)
Async XLA Ops:
  0.6 10.8 %copy-start = (bf16[128,2048]{1,0:T(8,128)(2,1)S(1)}, bf16[128,2048]{1,0:T(8,128)(2,1)}, u32[]{:S(2)}) copy-start(bf16[128,2048]{1,0:T(8,128)(2,1)} %param.5) | copy-start | bytes 1572868
  0.6 4.8 %copy-start.3 = (bf16[128,2048]{1,0:T(8,128)(2,1)S(1)}, bf16[128,2048]{1,0:T(8,128)(2,1)}, u32[]{:S(2)}) copy-start(bf16[128,2048]{1,0:T(8,128)(2,1)} %param.6) | copy-start | bytes 1572868
  2.1 15.1 %collective-permute-start.5 = (bf16[128,16,128]{0,2,1:T(8,128)(2,1)S(1)}, bf16[128,16,128]{0,2,1:T(8,128)(2,1)}, u32[]{:S(2)}, u32[]{:S(2)}) collective-permute-start(bf16[128,16,128]{0,2,1:T(8,128)(2,1)S(1)} %bitcast.185), channel_id=1, source_target_pairs={{0,1},{1,2},{2,3},{3,4},{4,5},{5,6},{6,7},{7,8},{8,9},{9,10},{10,1... | collective-permute-start | bytes 1572872 | tf_op jit(solution)/shard_map/ppermute | solution.py:13
  5.7 4.5 %copy-start.4 = (bf16[128,2048]{1,0:T(8,128)(2,1)S(1)}, bf16[128,2048]{1,0:T(8,128)(2,1)}, u32[]{:S(2)}) copy-start(bf16[128,2048]{1,0:T(8,128)(2,1)} %param.8) | copy-start | bytes 1572868
  6.7 21.8 %collective-permute-start = (bf16[128,16,128]{2,0,1:T(8,128)(2,1)}, bf16[128,16,128]{2,0,1:T(8,128)(2,1)}, u32[]{:S(2)}, u32[]{:S(2)}) collective-permute-start(bf16[128,16,128]{2,0,1:T(8,128)(2,1)} %copy.81), channel_id=1, source_target_pairs={{0,1},{1,2},{2,3},{3,4},{4,5},{5,6},{6,7},{7,8},{8,9},{9,10},{10,1... | collective-permute-start | bytes 1572872 | tf_op jit(solution)/shard_map/ppermute | solution.py:13
  17.1 22.6 %collective-permute-start.6 = (bf16[128,16,128]{0,2,1:T(8,128)(2,1)}, bf16[128,16,128]{0,2,1:T(8,128)(2,1)S(1)}, u32[]{:S(2)}, u32[]{:S(2)}) collective-permute-start(bf16[128,16,128]{0,2,1:T(8,128)(2,1)} %collective-permute-done.5), channel_id=1, source_target_pairs={{0,1},{1,2},{2,3},{3,4},{4,5},{5,6},{6,7},{7,8},{8,9},{9,10},{10,1... | collective-permute-start | bytes 1572872 | tf_op jit(solution)/shard_map/ppermute | solution.py:13
  28.5 22.5 %collective-permute-start.1 = (bf16[128,16,128]{2,0,1:T(8,128)(2,1)}, bf16[128,16,128]{2,0,1:T(8,128)(2,1)S(1)}, u32[]{:S(2)}, u32[]{:S(2)}) collective-permute-start(bf16[128,16,128]{2,0,1:T(8,128)(2,1)} %collective-permute-done), channel_id=1, source_target_pairs={{0,1},{1,2},{2,3},{3,4},{4,5},{5,6},{6,7},{7,8},{8,9},{9,10},{10,1... | collective-permute-start | bytes 1572872 | tf_op jit(solution)/shard_map/ppermute | solution.py:13
  39.7 22.4 %collective-permute-start.7 = (bf16[128,16,128]{0,2,1:T(8,128)(2,1)S(1)}, bf16[128,16,128]{0,2,1:T(8,128)(2,1)S(1)}, u32[]{:S(2)}, u32[]{:S(2)}) collective-permute-start(bf16[128,16,128]{0,2,1:T(8,128)(2,1)S(1)} %collective-permute-done.6), channel_id=1, source_target_pairs={{0,1},{1,2},{2,3},{3,4},{4,5},{5,6},{6,7},{7,8},{8,9},{9,10},{10,1... | collective-permute-start | bytes 1572872 | tf_op jit(solution)/shard_map/ppermute | solution.py:13
  50.9 22.4 %collective-permute-start.2 = (bf16[128,16,128]{2,0,1:T(8,128)(2,1)S(1)}, bf16[128,16,128]{2,0,1:T(8,128)(2,1)S(1)}, u32[]{:S(2)}, u32[]{:S(2)}) collective-permute-start(bf16[128,16,128]{2,0,1:T(8,128)(2,1)S(1)} %collective-permute-done.1), channel_id=1, source_target_pairs={{0,1},{1,2},{2,3},{3,4},{4,5},{5,6},{6,7},{7,8},{8,9},{9,10},{10,1... | collective-permute-start | bytes 1572872 | tf_op jit(solution)/shard_map/ppermute | solution.py:13
  62.1 22.5 %collective-permute-start.8 = (bf16[128,16,128]{0,2,1:T(8,128)(2,1)S(1)}, bf16[128,16,128]{0,2,1:T(8,128)(2,1)S(1)}, u32[]{:S(2)}, u32[]{:S(2)}) collective-permute-start(bf16[128,16,128]{0,2,1:T(8,128)(2,1)S(1)} %collective-permute-done.7), channel_id=1, source_target_pairs={{0,1},{1,2},{2,3},{3,4},{4,5},{5,6},{6,7},{7,8},{8,9},{9,10},{10,1... | collective-permute-start | bytes 1572872 | tf_op jit(solution)/shard_map/ppermute | solution.py:13
  73.3 22.5 %collective-permute-start.3 = (bf16[128,16,128]{2,0,1:T(8,128)(2,1)S(1)}, bf16[128,16,128]{2,0,1:T(8,128)(2,1)S(1)}, u32[]{:S(2)}, u32[]{:S(2)}) collective-permute-start(bf16[128,16,128]{2,0,1:T(8,128)(2,1)S(1)} %collective-permute-done.2), channel_id=1, source_target_pairs={{0,1},{1,2},{2,3},{3,4},{4,5},{5,6},{6,7},{7,8},{8,9},{9,10},{10,1... | collective-permute-start | bytes 1572872 | tf_op jit(solution)/shard_map/ppermute | solution.py:13
  84.5 39.1 %collective-permute-start.9 = (bf16[128,16,128]{0,2,1:T(8,128)(2,1)S(1)}, bf16[128,16,128]{0,2,1:T(8,128)(2,1)S(1)}, u32[]{:S(2)}, u32[]{:S(2)}) collective-permute-start(bf16[128,16,128]{0,2,1:T(8,128)(2,1)S(1)} %collective-permute-done.8), channel_id=1, source_target_pairs={{0,1},{1,2},{2,3},{3,4},{4,5},{5,6},{6,7},{7,8},{8,9},{9,10},{10,1... | collective-permute-start | bytes 1572872 | tf_op jit(solution)/shard_map/ppermute | solution.py:13
  95.8 22.1 %collective-permute-start.4 = (bf16[128,16,128]{2,0,1:T(8,128)(2,1)S(1)}, bf16[128,16,128]{2,0,1:T(8,128)(2,1)S(1)}, u32[]{:S(2)}, u32[]{:S(2)}) collective-permute-start(bf16[128,16,128]{2,0,1:T(8,128)(2,1)S(1)} %collective-permute-done.3), channel_id=1, source_target_pairs={{0,1},{1,2},{2,3},{3,4},{4,5},{5,6},{6,7},{7,8},{8,9},{9,10},{10,1... | collective-permute-start | bytes 1572872 | tf_op jit(solution)/shard_map/ppermute | solution.py:13
  124.5 0.8 copy-start.1
  126.5 24.6 %collective-permute-start.14 = (bf16[128,16,128]{0,2,1:T(8,128)(2,1)S(1)}, bf16[128,16,128]{0,2,1:T(8,128)(2,1)S(1)}, u32[]{:S(2)}, u32[]{:S(2)}) collective-permute-start(bf16[128,16,128]{0,2,1:T(8,128)(2,1)S(1)} %fusion.44), channel_id=1, source_target_pairs={{5,0},{6,1},{7,2},{8,3},{9,4},{10,5},{11,6},{12,7},{13,8},{14,9},{... | collective-permute-start | bytes 1572872 | tf_op jit(solution)/shard_map/ppermute | solution.py:13
  130.3 93.8 %collective-permute-start.13 = (bf16[128,16,128]{0,2,1:T(8,128)(2,1)S(1)}, bf16[128,16,128]{0,2,1:T(8,128)(2,1)S(1)}, u32[]{:S(2)}, u32[]{:S(2)}) collective-permute-start(bf16[128,16,128]{0,2,1:T(8,128)(2,1)S(1)} %fusion.45), channel_id=1, source_target_pairs={{4,0},{5,1},{6,2},{7,3},{8,4},{9,5},{10,6},{11,7},{12,8},{13,9},{1... | collective-permute-start | bytes 1572872 | tf_op jit(solution)/shard_map/ppermute | solution.py:13
  136.9 89.1 %collective-permute-start.12 = (bf16[128,16,128]{0,2,1:T(8,128)(2,1)S(1)}, bf16[128,16,128]{0,2,1:T(8,128)(2,1)S(1)}, u32[]{:S(2)}, u32[]{:S(2)}) collective-permute-start(bf16[128,16,128]{0,2,1:T(8,128)(2,1)S(1)} %fusion.46), channel_id=1, source_target_pairs={{3,0},{4,1},{5,2},{6,3},{7,4},{8,5},{9,6},{10,7},{11,8},{12,9},{13... | collective-permute-start | bytes 1572872 | tf_op jit(solution)/shard_map/ppermute | solution.py:13
  140.0 88.0 %collective-permute-start.11 = (bf16[128,16,128]{0,2,1:T(8,128)(2,1)S(1)}, bf16[128,16,128]{0,2,1:T(8,128)(2,1)S(1)}, u32[]{:S(2)}, u32[]{:S(2)}) collective-permute-start(bf16[128,16,128]{0,2,1:T(8,128)(2,1)S(1)} %fusion.47), channel_id=1, source_target_pairs={{2,0},{3,1},{4,2},{5,3},{6,4},{7,5},{8,6},{9,7},{10,8},{11,9},{12,... | collective-permute-start | bytes 1572872 | tf_op jit(solution)/shard_map/ppermute | solution.py:13
  144.4 85.5 %collective-permute-start.10 = (bf16[128,16,128]{0,2,1:T(8,128)(2,1)S(1)}, bf16[128,16,128]{0,2,1:T(8,128)(2,1)S(1)}, u32[]{:S(2)}, u32[]{:S(2)}) collective-permute-start(bf16[128,16,128]{0,2,1:T(8,128)(2,1)S(1)} %fusion.48), channel_id=1, source_target_pairs={{1,0},{2,1},{3,2},{4,3},{5,4},{6,5},{7,6},{8,7},{9,8},{10,9},{11,1... | collective-permute-start | bytes 1572872 | tf_op jit(solution)/shard_map/ppermute | solution.py:13
  151.1 81.1 %copy-start.5 = (bf16[128,16,128]{0,2,1:T(8,128)(2,1)}, bf16[128,16,128]{0,2,1:T(8,128)(2,1)S(1)}, u32[]{:S(2)}) copy-start(bf16[128,16,128]{0,2,1:T(8,128)(2,1)S(1)} %collective-permute-done.14) | copy-start | bytes 1572868
  151.2 85.6 %collective-permute-start.19 = (bf16[128,16,128]{0,2,1:T(8,128)(2,1)}, bf16[128,16,128]{0,2,1:T(8,128)(2,1)}, u32[]{:S(2)}, u32[]{:S(2)}) collective-permute-start(bf16[128,16,128]{0,2,1:T(8,128)(2,1)} %fusion.53), channel_id=1, source_target_pairs={{5,0},{6,1},{7,2},{8,3},{9,4},{10,5},{11,6},{12,7},{13,8},{14,9},{... | collective-permute-start | bytes 1572872 | tf_op jit(solution)/shard_map/ppermute | solution.py:13
  224.1 8.1 %copy-start.6 = (bf16[128,16,128]{0,2,1:T(8,128)(2,1)}, bf16[128,16,128]{0,2,1:T(8,128)(2,1)S(1)}, u32[]{:S(2)}) copy-start(bf16[128,16,128]{0,2,1:T(8,128)(2,1)S(1)} %collective-permute-done.13) | copy-start | bytes 1572868
  224.1 44.7 %collective-permute-start.18 = (bf16[128,16,128]{0,2,1:T(8,128)(2,1)}, bf16[128,16,128]{0,2,1:T(8,128)(2,1)}, u32[]{:S(2)}, u32[]{:S(2)}) collective-permute-start(bf16[128,16,128]{0,2,1:T(8,128)(2,1)} %fusion.52), channel_id=1, source_target_pairs={{4,0},{5,1},{6,2},{7,3},{8,4},{9,5},{10,6},{11,7},{12,8},{13,9},{1... | collective-permute-start | bytes 1572872 | tf_op jit(solution)/shard_map/ppermute | solution.py:13
  226.1 6.2 %copy-start.7 = (bf16[128,16,128]{0,2,1:T(8,128)(2,1)}, bf16[128,16,128]{0,2,1:T(8,128)(2,1)S(1)}, u32[]{:S(2)}) copy-start(bf16[128,16,128]{0,2,1:T(8,128)(2,1)S(1)} %collective-permute-done.12) | copy-start | bytes 1572868
  226.1 71.0 %collective-permute-start.17 = (bf16[128,16,128]{0,2,1:T(8,128)(2,1)}, bf16[128,16,128]{0,2,1:T(8,128)(2,1)}, u32[]{:S(2)}, u32[]{:S(2)}) collective-permute-start(bf16[128,16,128]{0,2,1:T(8,128)(2,1)} %fusion.51), channel_id=1, source_target_pairs={{3,0},{4,1},{5,2},{6,3},{7,4},{8,5},{9,6},{10,7},{11,8},{12,9},{13... | collective-permute-start | bytes 1572872 | tf_op jit(solution)/shard_map/ppermute | solution.py:13
  228.0 4.3 %copy-start.8 = (bf16[128,16,128]{0,2,1:T(8,128)(2,1)}, bf16[128,16,128]{0,2,1:T(8,128)(2,1)S(1)}, u32[]{:S(2)}) copy-start(bf16[128,16,128]{0,2,1:T(8,128)(2,1)S(1)} %collective-permute-done.11) | copy-start | bytes 1572868
  228.0 69.1 %collective-permute-start.16 = (bf16[128,16,128]{0,2,1:T(8,128)(2,1)}, bf16[128,16,128]{0,2,1:T(8,128)(2,1)}, u32[]{:S(2)}, u32[]{:S(2)}) collective-permute-start(bf16[128,16,128]{0,2,1:T(8,128)(2,1)} %fusion.50), channel_id=1, source_target_pairs={{2,0},{3,1},{4,2},{5,3},{6,4},{7,5},{8,6},{9,7},{10,8},{11,9},{12,... | collective-permute-start | bytes 1572872 | tf_op jit(solution)/shard_map/ppermute | solution.py:13
  230.0 2.3 copy-start.9
  230.0 67.2 %collective-permute-start.15 = (bf16[128,16,128]{0,2,1:T(8,128)(2,1)}, bf16[128,16,128]{0,2,1:T(8,128)(2,1)}, u32[]{:S(2)}, u32[]{:S(2)}) collective-permute-start(bf16[128,16,128]{0,2,1:T(8,128)(2,1)} %fusion.49), channel_id=1, source_target_pairs={{1,0},{2,1},{3,2},{4,3},{5,4},{6,5},{7,6},{8,7},{9,8},{10,9},{11,1... | collective-permute-start | bytes 1572872 | tf_op jit(solution)/shard_map/ppermute | solution.py:13
  232.3 1.0 copy-start.2
where the time goes:
time: 301 us; the launch traced here: 300 us
  waiting for transfers between devices  167 us (55%)
  starting transfers between devices  96.8 us (32%)
  matrix products  27.6 us (9%)
  local copies, waits for them, and re-layouts  6.83 us (2%)
    ppermute x20, waiting for transfers between devices, shifted(): lax.ppermute(value, axis, [(source, source + steps) for source in range(f...  167 us
    ppermute x20, starting transfers between devices, shifted(): lax.ppermute(value, axis, [(source, source + steps) for source in range(f...  96.8 us
    dot_general x6, matrix products, pair_grads(): jnp.einsum('hqk,qhd->khd', probs_low, out_grad, preferred_element_type=jn...  8.8 us
  transfers between devices with their start and end apart: 20, of which 12 were waited for; matrix products, arithmetic and copies ran while one was open for 9% of the time, Pallas kernels for 0%

commit v1 on v0

v1 whole, which is shorter than its diff:
```python
import functools

import jax
import jax.numpy as jnp
from jax import lax
from jax.experimental import pallas as pl
from jax.experimental.pallas import tpu as pltpu
from jax.sharding import PartitionSpec as P

HD = 128
LINE = 4
GROUP = 1
MESH = pl.DeviceIdType.MESH
NT = (((1,), (1,)), ((), ()))
NN = (((1,), (0,)), ((), ()))
TN = (((0,), (0,)), ((), ()))


def dot(a, b, dims):
    return lax.dot_general(a, b, dims, preferred_element_type=jnp.float32)


def kernel(
    sizes, window, q_ref, k_ref, v_ref, g_ref, dq_ref, dk_ref, dv_ref,
    qd, kv, slot, rout, acc, fin, w_s, p_s,
    xsend, xrecv, xloc, fsend, frecv, rsend, rrecv, osend, orecv, oloc,
):
    outer, inner, tok, heads = sizes
    half = heads // 2
    chunks = half // GROUP
    wide = GROUP * HD
    scale = HD ** -0.5
    total = outer * inner
    lines = total // (2 * LINE)
    me = lax.axis_index("outer") * inner + lax.axis_index("inner")
    x = lax.rem(me, 2)
    pair = me // 2
    z = lax.rem(pair, LINE)
    line = pair // LINE

    def dev(to_line, to_z, to_x):
        s = (to_line * LINE + to_z) * 2 + to_x
        return (s // inner, lax.rem(s, inner))

    partner = dev(line, z, 1 - x)
    up = dev(line, lax.rem(z + 1, LINE), x)
    down = dev(line, lax.rem(z + LINE - 1, LINE), x)
    ahead = dev(lax.rem(line + 1, lines), lax.rem(z + LINE - 1, LINE), x)
    behind = dev(lax.rem(line + lines - 1, lines), lax.rem(z + 1, LINE), x)
    low = z >= 1
    high = z <= LINE - 2

    ins = (k_ref, v_ref, q_ref, g_ref)
    outs = (dq_ref, dk_ref, dv_ref)

    def cols(side, c):
        return pl.ds(pl.multiple_of((side * half + c * GROUP) * HD, HD), wide)

    my_rows = pl.ds(pl.multiple_of(x * tok, tok), tok)
    other_rows = pl.ds(pl.multiple_of((1 - x) * tok, tok), tok)

    def landing(i, c):
        return kv.at[0, c, i, my_rows, :] if i < 2 else qd.at[c, i - 2, my_rows, :]

    def local_in(i, c):
        return pltpu.make_async_copy(ins[i].at[:, cols(x, c)], landing(i, c), xloc.at[c, i])

    def cross_in(i, c):
        return pltpu.make_async_remote_copy(
            ins[i].at[:, cols(1 - x, c)], landing(i, c), xsend.at[c, i], xrecv.at[c, i],
            device_id=partner, device_id_type=MESH)

    def local_out(i, c):
        return pltpu.make_async_copy(
            fin.at[c, i, my_rows, :], outs[i].at[:, cols(x, c)], oloc.at[c, i])

    def cross_out(i, c):
        return pltpu.make_async_remote_copy(
            fin.at[c, i, other_rows, :], outs[i].at[:, cols(x, c)], osend.at[c, i],
            orecv.at[c, i], device_id=partner, device_id_type=MESH)

    def forward(c, src, dst, sem, to):
        return pltpu.make_async_remote_copy(
            kv.at[src, c], kv.at[dst, c], fsend.at[c, sem], frecv.at[c, dst - 1],
            device_id=to, device_id_type=MESH)

    def back(c, d, dst, to):
        return pltpu.make_async_remote_copy(
            rout.at[d - 1, c], slot.at[dst, c], rsend.at[c, d - 1], rrecv.at[c, dst],
            device_id=to, device_id_type=MESH)

    def arrived(c, d):
        forward(c, 0, d, 0, up).wait_recv()

    def returned(c, dst):
        back(c, 1, dst, up).wait_recv()

    def every_chunk(body):
        def step(c, carry):
            body(c)
            return carry
        lax.fori_loop(0, chunks, step, 0)

    @every_chunk
    def _(c):
        for i in range(4):
            local_in(i, c).start()

    barrier = pltpu.get_barrier_semaphore()
    pl.semaphore_signal(barrier, inc=1, device_id=partner, device_id_type=MESH)
    for cond, targets in ((high, (up, behind)), (low, (down, ahead))):
        @pl.when(cond)
        def _():
            for target in targets:
                pl.semaphore_signal(barrier, inc=1, device_id=target, device_id_type=MESH)
    pl.semaphore_wait(barrier, 1 + 2 * high.astype(jnp.int32) + 2 * low.astype(jnp.int32))

    @every_chunk
    def _(c):
        for i in range(4):
            cross_in(i, c).start()

    def when(*conds):
        return pl.when(functools.reduce(jnp.logical_and, conds))

    def stage_a(c):
        for i in range(2):
            local_in(i, c).wait()
            cross_in(i, c).wait_recv()

        @when(high)
        def _():
            forward(c, 0, 1, 0, up).start()

        @when(low)
        def _():
            forward(c, 0, 3, 1, ahead).start()

    def stage_b1(c):
        @when(low)
        def _():
            arrived(c, 1)

            @when(high)
            def _():
                forward(c, 1, 2, 2, up).start()

        @when(high)
        def _():
            arrived(c, 3)

            @when(low)
            def _():
                forward(c, 3, 2, 3, down).start()

    def stage_b2(c):
        arrived(c, 2)

        @when(z == 2)
        def _():
            forward(c, 2, 3, 4, up).start()

        @when(z == 1)
        def _():
            forward(c, 2, 1, 4, down).start()

    def stage_c(c):
        for i in range(2, 4):
            local_in(i, c).wait()
            cross_in(i, c).wait_recv()

        @when(z == LINE - 1)
        def _():
            arrived(c, 3)

        @when(z == 0)
        def _():
            arrived(c, 1)

        width = window[0]
        size = 2 * tok
        for h in range(GROUP):
            hs = slice(h * HD, (h + 1) * HD)
            query, grad = qd[c, 0, :, hs], qd[c, 1, :, hs]
            norm = jnp.zeros((1, size), jnp.float32)
            mixed = jnp.zeros((1, size), jnp.float32)
            for d in range(4):
                rows, top = (size, 0) if d < 3 else (tok, tok)
                key, value = kv[d, c, 0, top:, hs], kv[d, c, 1, top:, hs]
                logits = dot(key, query[:rows], NT) * scale
                shape = (rows, rows)
                delta = (
                    lax.broadcasted_iota(jnp.int32, shape, 1)
                    - lax.broadcasted_iota(jnp.int32, shape, 0)
                    + (d * size - top)
                )
                reach = jnp.where(pair >= d, width, 0)
                allowed = (delta >= 0) & (delta < reach) if d == 0 else delta < reach
                weights = jnp.where(allowed, jnp.exp(logits), 0.0)
                prob_grad = dot(value, grad[:rows], NT)
                w_s[d, :rows, :rows] = weights
                p_s[d, :rows, :rows] = prob_grad
                norm_part = jnp.sum(weights, axis=0, keepdims=True)
                mixed_part = jnp.sum(weights * prob_grad, axis=0, keepdims=True)
                if d == 3:
                    rest = jnp.zeros((1, size - tok), jnp.float32)
                    norm_part = jnp.concatenate([norm_part, rest], axis=1)
                    mixed_part = jnp.concatenate([mixed_part, rest], axis=1)
                norm = norm + norm_part
                mixed = mixed + mixed_part
            inverse = 1.0 / norm
            centre = mixed * inverse
            query_total = jnp.zeros((size, HD), jnp.float32)
            for d in range(4):
                rows, top = (size, 0) if d < 3 else (tok, tok)
                probs = w_s[d, :rows, :rows] * inverse[:, :rows]
                logit_grad = probs * (p_s[d, :rows, :rows] - centre[:, :rows])
                logit_grad = logit_grad.astype(jnp.bfloat16)
                acc[c, d, 1, top:, hs] = dot(probs.astype(jnp.bfloat16), grad[:rows], NN)
                acc[c, d, 0, top:, hs] = dot(logit_grad, query[:rows], NN) * scale
                part = dot(logit_grad, kv[d, c, 0, top:, hs], TN)
                if d == 3:
                    acc[c, d, :, :top, hs] = jnp.zeros((2, top, HD), jnp.float32)
                    part = jnp.concatenate([part, jnp.zeros((size - tok, HD), jnp.float32)], axis=0)
                query_total = query_total + part
            fin[c, 0, :, hs] = (query_total * scale).astype(jnp.bfloat16)
        local_out(0, c).start()
        cross_out(0, c).start()

        @when(z == LINE - 1)
        def _():
            rout[2, c] = acc[c, 3].astype(jnp.bfloat16)
            back(c, 3, 2, down).start()

        @when(z == 0)
        def _():
            rout[0, c] = acc[c, 1].astype(jnp.bfloat16)
            back(c, 1, 2, up).start()

    def fold(c, d, has_child, source):
        @when(has_child)
        def _():
            returned(c, source)
            rout[d - 1, c] = (acc[c, d] + slot[source, c].astype(jnp.float32)).astype(jnp.bfloat16)

        @when(jnp.logical_not(has_child))
        def _():
            rout[d - 1, c] = acc[c, d].astype(jnp.bfloat16)

    def stage_r2(c):
        fold(c, 2, jnp.logical_and(low, high), 2)

        @when(z >= 2)
        def _():
            back(c, 2, 1, down).start()

        @when(z < 2)
        def _():
            back(c, 2, 3, up).start()

    def stage_r1(c):
        @when(low)
        def _():
            fold(c, 1, high, 1)
            back(c, 1, 0, down).start()

        @when(high)
        def _():
            fold(c, 3, low, 3)
            back(c, 3, 4, behind).start()

    def stage_r0(c):
        @when(high)
        def _():
            returned(c, 0)
            acc[c, 0] = acc[c, 0] + slot[0, c].astype(jnp.float32)

        @when(low)
        def _():
            returned(c, 4)
            acc[c, 0] = acc[c, 0] + slot[4, c].astype(jnp.float32)

        fin[c, 1:] = acc[c, 0].astype(jnp.bfloat16)
        for i in range(1, 3):
            local_out(i, c).start()
            cross_out(i, c).start()

    stages = (stage_a, stage_b1, stage_b2, stage_c, stage_r2, stage_r1, stage_r0)

    def tick(t, carry):
        for lag, stage in enumerate(stages):
            c = t - lag

            @when(c >= 0, c < chunks)
            def _():
                stage(c)
        return carry

    lax.fori_loop(0, chunks + len(stages) - 1, tick, 0)

    @every_chunk
    def _(c):
        for i in range(4):
            cross_in(i, c).wait_send()
        for i in range(3):
            local_out(i, c).wait()
            cross_out(i, c).wait()

        @when(high)
        def _():
            forward(c, 0, 1, 0, up).wait_send()

        @when(low)
        def _():
            forward(c, 0, 3, 1, ahead).wait_send()

        @when(low, high)
        def _():
            forward(c, 1, 2, 2, up).wait_send()
            forward(c, 3, 2, 3, down).wait_send()
            forward(c, 2, 3, 4, up).wait_send()
        for d in range(1, 4):
            back(c, d, 0, up).wait_send()


def per_device(queries, keys, values, grad_out, window):
    outer, inner = lax.axis_size("outer"), lax.axis_size("inner")
    tok, columns = queries.shape
    heads = columns // HD
    half = heads // 2
    chunks = half // GROUP
    wide = GROUP * HD
    size = 2 * tok
    low, full = jnp.bfloat16, jnp.float32
    vmem = pl.BlockSpec(memory_space=pltpu.VMEM)
    block = (chunks, 2, size, wide)
    sems = (4, 4, 4, 5, 3, 3, 5, 3, 3, 3)
    return pl.pallas_call(
        functools.partial(kernel, (outer, inner, tok, heads)),
        out_shape=[jax.ShapeDtypeStruct((tok, columns), low)] * 3,
        in_specs=[pl.BlockSpec(memory_space=pltpu.SMEM)] + [vmem] * 4,
        out_specs=[vmem] * 3,
        scratch_shapes=[
            pltpu.VMEM(block, low),
            pltpu.VMEM((4,) + block, low),
            pltpu.VMEM((5,) + block, low),
            pltpu.VMEM((3,) + block, low),
            pltpu.VMEM((chunks, 4, 2, size, wide), full),
            pltpu.VMEM((chunks, 3, size, wide), low),
            pltpu.VMEM((4, size, size), full),
            pltpu.VMEM((4, size, size), full),
        ] + [pltpu.SemaphoreType.DMA((chunks, n)) for n in sems],
        compiler_params=pltpu.CompilerParams(
            collective_id=0, has_side_effects=True, vmem_limit_bytes=56 * 2**20
        ),
    )(window, queries, keys, values, grad_out)


def solution(mesh):
    rows = P(("outer", "inner"), None)
    return jax.shard_map(
        per_device,
        mesh=mesh,
        in_specs=(rows, rows, rows, rows, P()),
        out_specs=(rows, rows, rows),
        check_vma=False,
    )
```

time: 301 us -> 123 us (0.41)
  the two profiles are of different devices: /device:TPU:27 before, /device:TPU:0 now
where the time goes in v1:
time: 123 us; the launch traced here: 122 us
  Pallas kernels  117 us (95%)
  local copies, waits for them, and re-layouts  3.97 us (3%)
  between operations  1.3 us (1%)
    pallas_call x1, Pallas kernels, per_device(): pl.pallas_call(functools.partial(kernel, (outer, inner, tok, heads)), out...  117 us
    unnamed x7, local copies, waits for them, and re-layouts  3.97 us

profile of v1, /device:TPU:0, one launch (start us, length us, event | category | flops | bytes accessed | tf_op | source)
XLA Modules:
  0.0 122.1 jit_solution(10161433227458572802)
XLA Ops:
  1.3 116.8 %shard_map.76 = (bf16[128,2048]{1,0:T(8,128)(2,1)}, bf16[128,2048]{1,0:T(8,128)(2,1)}, bf16[128,2048]{1,0:T(8,128)(2,1)}) custom-call(s32[1]{0:T(128)S(6)} %copy.11.window, bf16[128,2048]{1,0:T(8,128)(2,1)} %q_ref.1, bf16[128,2048]{1,0:T(8,128)(2,1)} %k_ref.1, bf16[128,2048]{1,0:T(8,128)(2,1)} %v_ref.1, bf16[128,2048]{1,0:T(8,128)(2,1)} %g_ref.1), custom_call_target="tpu_custom_call" | custom-call | tf_op jit(solution)/shard_map/pallas_call | solution.py:338
  118.1 0.0 copy-start.1
  118.1 1.9 %copy.12 = bf16[128,2048]{1,0:T(8,128)(2,1)} copy(bf16[128,2048]{1,0:T(8,128)(2,1)} %get-tuple-element.6) | data formatting | bytes 1048576
  120.0 0.0 copy-done.1
  120.0 0.0 copy-start
  120.0 0.8 copy.13
  120.8 0.4 copy-done
  121.3 0.8 copy.14
Async XLA Ops:
  118.1 2.0 %copy-start.1 = (bf16[128,2048]{1,0:T(8,128)(2,1)S(1)}, bf16[128,2048]{1,0:T(8,128)(2,1)}, u32[]{:S(2)}) copy-start(bf16[128,2048]{1,0:T(8,128)(2,1)} %get-tuple-element.7) | copy-start | bytes 1572868
  120.0 1.2 %copy-start = (bf16[128,2048]{1,0:T(8,128)(2,1)S(1)}, bf16[128,2048]{1,0:T(8,128)(2,1)}, u32[]{:S(2)}) copy-start(bf16[128,2048]{1,0:T(8,128)(2,1)} %get-tuple-element.8) | copy-start | bytes 1572868

commit v2 on v1

v2 whole, which is shorter than its diff:
```python
import functools

import jax
import jax.numpy as jnp
from jax import lax
from jax.experimental import pallas as pl
from jax.experimental.pallas import tpu as pltpu
from jax.sharding import PartitionSpec as P

HD = 128
LINE = 4
MESH = pl.DeviceIdType.MESH
NT = (((1,), (1,)), ((), ()))
NN = (((1,), (0,)), ((), ()))
TN = (((0,), (0,)), ((), ()))


def dot(a, b, dims):
    return lax.dot_general(a, b, dims, preferred_element_type=jnp.float32)


def kernel(
    sizes, window, q_ref, k_ref, v_ref, g_ref, dq_ref, dk_ref, dv_ref,
    qg, kv, slot, rout, acc, fin, w_s, p_s, part_out, part_in, whole_out, whole_in,
    xsend, xrecv, xloc, fsend, frecv, rsend, rrecv, osend, orecv, oloc, psend, precv, tsend, trecv,
):
    outer, inner, tok, heads = sizes
    half = heads // 2
    chunks = half
    size = 2 * tok
    scale = HD ** -0.5
    total = outer * inner
    pairs = total // 2
    me = lax.axis_index("outer") * inner + lax.axis_index("inner")
    x = lax.rem(me, 2)
    pair = me // 2
    z = LINE - 1 - lax.rem(pair, LINE)

    def dev(steps, to_x):
        s = lax.rem(pair + steps + pairs, pairs) * 2 + to_x
        return (s // inner, lax.rem(s, inner))

    partner = dev(0, 1 - x)
    up = dev(-1, x)
    down = dev(1, x)
    ahead = dev(-3, x)
    behind = dev(3, x)
    low = z >= 1
    high = z <= LINE - 2

    ins = (q_ref, g_ref, k_ref, v_ref)
    outs = (dq_ref, dk_ref, dv_ref)

    def cols(side, c):
        return pl.ds(pl.multiple_of((side * half + c) * HD, HD), HD)

    my_rows = pl.ds(pl.multiple_of(x * tok, tok), tok)
    other_rows = pl.ds(pl.multiple_of((1 - x) * tok, tok), tok)

    def landing(i, c):
        return qg.at[0, c, i, my_rows, :] if i < 2 else kv.at[c, i - 2, my_rows, :]

    def local_in(i, c):
        return pltpu.make_async_copy(ins[i].at[:, cols(x, c)], landing(i, c), xloc.at[c, i])

    def cross_in(i, c):
        return pltpu.make_async_remote_copy(
            ins[i].at[:, cols(1 - x, c)], landing(i, c), xsend.at[c, i], xrecv.at[c, i],
            device_id=partner, device_id_type=MESH)

    def local_out(i, c):
        return pltpu.make_async_copy(
            fin.at[c, i, my_rows, :], outs[i].at[:, cols(x, c)], oloc.at[c, i])

    def cross_out(i, c):
        return pltpu.make_async_remote_copy(
            fin.at[c, i, other_rows, :], outs[i].at[:, cols(x, c)], osend.at[c, i],
            orecv.at[c, i], device_id=partner, device_id_type=MESH)

    def forward(c, src, dst, sem, to):
        return pltpu.make_async_remote_copy(
            qg.at[src, c], qg.at[dst, c], fsend.at[c, sem], frecv.at[c, dst - 1],
            device_id=to, device_id_type=MESH)

    def back(c, d, dst, to):
        return pltpu.make_async_remote_copy(
            rout.at[d - 1, c], slot.at[dst, c], rsend.at[c, d - 1], rrecv.at[c, dst],
            device_id=to, device_id_type=MESH)

    def partial(c, d):
        return pltpu.make_async_remote_copy(
            part_out.at[c, d], part_in.at[c, d], psend.at[c, d - 1], precv.at[c, d - 1],
            device_id=dev(d, x), device_id_type=MESH)

    def totals(c, d):
        return pltpu.make_async_remote_copy(
            whole_out.at[c], whole_in.at[c, d], tsend.at[c, d - 1], trecv.at[c, d - 1],
            device_id=dev(-d, x), device_id_type=MESH)

    def arrived(c, d):
        forward(c, 0, d, 0, up).wait_recv()

    def returned(c, dst):
        back(c, 1, dst, up).wait_recv()

    def every_chunk(body):
        def step(c, carry):
            body(c)
            return carry
        lax.fori_loop(0, chunks, step, 0)

    @every_chunk
    def _(c):
        for i in range(4):
            local_in(i, c).start()

    barrier = pltpu.get_barrier_semaphore()
    for target in [partner] + [dev(d, x) for d in (-3, -2, -1, 1, 2, 3)]:
        pl.semaphore_signal(barrier, inc=1, device_id=target, device_id_type=MESH)
    pl.semaphore_wait(barrier, 7)

    @every_chunk
    def _(c):
        for i in range(4):
            cross_in(i, c).start()

    def when(*conds):
        return pl.when(functools.reduce(jnp.logical_and, conds))

    def stage_a(c):
        for i in range(2):
            local_in(i, c).wait()
            cross_in(i, c).wait_recv()

        @when(high)
        def _():
            forward(c, 0, 1, 0, up).start()

        @when(low)
        def _():
            forward(c, 0, 3, 1, ahead).start()

    def stage_b1(c):
        @when(low)
        def _():
            arrived(c, 1)

            @when(high)
            def _():
                forward(c, 1, 2, 2, up).start()

        @when(high)
        def _():
            arrived(c, 3)

            @when(low)
            def _():
                forward(c, 3, 2, 3, down).start()

    def stage_b2(c):
        arrived(c, 2)

        @when(z == 2)
        def _():
            forward(c, 2, 3, 4, up).start()

        @when(z == 1)
        def _():
            forward(c, 2, 1, 4, down).start()

    def stage_c(c):
        for i in range(2, 4):
            local_in(i, c).wait()
            cross_in(i, c).wait_recv()

        @when(z == LINE - 1)
        def _():
            arrived(c, 3)

        @when(z == 0)
        def _():
            arrived(c, 1)

        width = window[0]
        key_all, value_all = kv[c, 0], kv[c, 1]
        for d in range(4):
            rows, top = (size, 0) if d < 3 else (tok, tok)
            logits = dot(key_all[top:], qg[d, c, 0, :rows, :], NT) * scale
            shape = (rows, rows)
            delta = (
                lax.broadcasted_iota(jnp.int32, shape, 1)
                - lax.broadcasted_iota(jnp.int32, shape, 0)
                + (d * size - top)
            )
            reach = jnp.where(pair + d < pairs, width, 0)
            allowed = (delta >= 0) & (delta < reach) if d == 0 else delta < reach
            weights = jnp.where(allowed, jnp.exp(logits), 0.0)
            prob_grad = dot(value_all[top:], qg[d, c, 1, :rows, :], NT)
            w_s[c, d, :rows, :rows] = weights
            p_s[c, d, :rows, :rows] = prob_grad
            norm = jnp.sum(weights, axis=0, keepdims=True)
            mixed = jnp.sum(weights * prob_grad, axis=0, keepdims=True)
            if d == 3:
                part_out[c, d] = jnp.zeros((2, size), jnp.float32)
            part_out[c, d, 0:1, :rows] = norm
            part_out[c, d, 1:2, :rows] = mixed
            if d > 0:
                partial(c, d).start()

    def stage_s1(c):
        for d in range(1, 4):
            partial(c, d).wait_recv()
        sums = part_out[c, 0] + part_in[c, 1] + part_in[c, 2] + part_in[c, 3]
        inverse = 1.0 / sums[0:1]
        whole_out[c, 0:1] = inverse
        whole_out[c, 1:2] = sums[1:2] * inverse
        for d in range(1, 4):
            totals(c, d).start()

    def stage_s2(c):
        for d in range(1, 4):
            totals(c, d).wait_recv()
        key_all = kv[c, 0]
        key_total = jnp.zeros((size, HD), jnp.float32)
        value_total = jnp.zeros((size, HD), jnp.float32)
        for d in (3, 2, 1, 0):
            rows, top = (size, 0) if d < 3 else (tok, tok)
            stats = whole_in[c, d] if d else whole_out[c]
            probs = w_s[c, d, :rows, :rows] * stats[0:1, :rows]
            logit_grad = probs * (p_s[c, d, :rows, :rows] - stats[1:2, :rows])
            logit_grad = logit_grad.astype(jnp.bfloat16)
            value_part = dot(probs.astype(jnp.bfloat16), qg[d, c, 1, :rows, :], NN)
            key_part = dot(logit_grad, qg[d, c, 0, :rows, :], NN)
            if d == 3:
                acc[c, d, rows:, :] = jnp.zeros((size - rows, HD), jnp.float32)
                rest = jnp.zeros((top, HD), jnp.float32)
                value_part = jnp.concatenate([rest, value_part], axis=0)
                key_part = jnp.concatenate([rest, key_part], axis=0)
            value_total = value_total + value_part
            key_total = key_total + key_part
            acc[c, d, :rows, :] = dot(logit_grad, key_all[top:], TN) * scale
        fin[c, 1] = (key_total * scale).astype(jnp.bfloat16)
        fin[c, 2] = value_total.astype(jnp.bfloat16)

        @when(z == LINE - 1)
        def _():
            rout[2, c] = acc[c, 3].astype(jnp.bfloat16)
            back(c, 3, 2, down).start()

        @when(z == 0)
        def _():
            rout[0, c] = acc[c, 1].astype(jnp.bfloat16)
            back(c, 1, 2, up).start()

        for i in range(1, 3):
            local_out(i, c).start()
            cross_out(i, c).start()

    def fold(c, d, has_child, source):
        @when(has_child)
        def _():
            returned(c, source)
            rout[d - 1, c] = (acc[c, d] + slot[source, c].astype(jnp.float32)).astype(jnp.bfloat16)

        @when(jnp.logical_not(has_child))
        def _():
            rout[d - 1, c] = acc[c, d].astype(jnp.bfloat16)

    def stage_r2(c):
        fold(c, 2, jnp.logical_and(low, high), 2)

        @when(z >= 2)
        def _():
            back(c, 2, 1, down).start()

        @when(z < 2)
        def _():
            back(c, 2, 3, up).start()

    def stage_r1(c):
        @when(low)
        def _():
            fold(c, 1, high, 1)
            back(c, 1, 0, down).start()

        @when(high)
        def _():
            fold(c, 3, low, 3)
            back(c, 3, 4, behind).start()

    def stage_r0(c):
        @when(high)
        def _():
            returned(c, 0)
            acc[c, 0] = acc[c, 0] + slot[0, c].astype(jnp.float32)

        @when(low)
        def _():
            returned(c, 4)
            acc[c, 0] = acc[c, 0] + slot[4, c].astype(jnp.float32)

        fin[c, 0] = acc[c, 0].astype(jnp.bfloat16)
        local_out(0, c).start()
        cross_out(0, c).start()

    stages = (
        stage_a, stage_b1, stage_b2, stage_c, stage_s1, stage_s2, stage_r2, stage_r1, stage_r0
    )

    def tick(t, carry):
        for lag, stage in enumerate(stages):
            c = t - lag

            @when(c >= 0, c < chunks)
            def _():
                stage(c)
        return carry

    lax.fori_loop(0, chunks + len(stages) - 1, tick, 0)

    @every_chunk
    def _(c):
        for i in range(4):
            cross_in(i, c).wait_send()
        for i in range(3):
            local_out(i, c).wait()
            cross_out(i, c).wait()

        @when(high)
        def _():
            forward(c, 0, 1, 0, up).wait_send()

        @when(low)
        def _():
            forward(c, 0, 3, 1, ahead).wait_send()

        @when(low, high)
        def _():
            forward(c, 1, 2, 2, up).wait_send()
            forward(c, 3, 2, 3, down).wait_send()
            forward(c, 2, 3, 4, up).wait_send()
        for d in range(1, 4):
            back(c, d, 0, up).wait_send()
            partial(c, d).wait_send()
            totals(c, d).wait_send()


def per_device(queries, keys, values, grad_out, window):
    outer, inner = lax.axis_size("outer"), lax.axis_size("inner")
    tok, columns = queries.shape
    heads = columns // HD
    chunks = heads // 2
    size = 2 * tok
    low, full = jnp.bfloat16, jnp.float32
    vmem = pl.BlockSpec(memory_space=pltpu.VMEM)
    block = (chunks, 2, size, HD)
    sums = (chunks, size, HD)
    sems = (4, 4, 4, 5, 3, 3, 5, 3, 3, 3, 3, 3, 3, 3)
    return pl.pallas_call(
        functools.partial(kernel, (outer, inner, tok, heads)),
        out_shape=[jax.ShapeDtypeStruct((tok, columns), low)] * 3,
        in_specs=[pl.BlockSpec(memory_space=pltpu.SMEM)] + [vmem] * 4,
        out_specs=[vmem] * 3,
        scratch_shapes=[
            pltpu.VMEM((4,) + block, low),
            pltpu.VMEM(block, low),
            pltpu.VMEM((5,) + sums, low),
            pltpu.VMEM((3,) + sums, low),
            pltpu.VMEM((chunks, 4, size, HD), full),
            pltpu.VMEM((chunks, 3, size, HD), low),
            pltpu.VMEM((chunks, 4, size, size), full),
            pltpu.VMEM((chunks, 4, size, size), full),
            pltpu.VMEM((chunks, 4, 2, size), full),
            pltpu.VMEM((chunks, 4, 2, size), full),
            pltpu.VMEM((chunks, 2, size), full),
            pltpu.VMEM((chunks, 4, 2, size), full),
        ] + [pltpu.SemaphoreType.DMA((chunks, n)) for n in sems],
        compiler_params=pltpu.CompilerParams(
            collective_id=0, has_side_effects=True, vmem_limit_bytes=56 * 2**20
        ),
    )(window, queries, keys, values, grad_out)


def solution(mesh):
    rows = P(("outer", "inner"), None)
    return jax.shard_map(
        per_device,
        mesh=mesh,
        in_specs=(rows, rows, rows, rows, P()),
        out_specs=(rows, rows, rows),
        check_vma=False,
    )
```

time: 123 us -> 118 us (0.959)
  Pallas kernels: 117 us -> 112 us
    pallas_call x1, Pallas kernels: 117 us -> 112 us  [per_device(): pl.pallas_call(functools.partial(kernel, (outer, inner, tok, heads)), out...]
where the time goes in v2:
time: 118 us
  Pallas kernels  112 us (95%)
  local copies, waits for them, and re-layouts  3.97 us (3%)
  between operations  1.3 us (1%)
    pallas_call x1, Pallas kernels, per_device(): pl.pallas_call(functools.partial(kernel, (outer, inner, tok, heads)), out...  112 us
    unnamed x7, local copies, waits for them, and re-layouts  3.97 us

profile of v2, /device:TPU:0, one launch (start us, length us, event | category | flops | bytes accessed | tf_op | source)
XLA Modules:
  0.0 117.7 jit_solution(14920982232462238722)
XLA Ops:
  1.3 112.4 %shard_map.76 = (bf16[128,2048]{1,0:T(8,128)(2,1)}, bf16[128,2048]{1,0:T(8,128)(2,1)}, bf16[128,2048]{1,0:T(8,128)(2,1)}) custom-call(s32[1]{0:T(128)S(6)} %copy.11.window, bf16[128,2048]{1,0:T(8,128)(2,1)} %q_ref.1, bf16[128,2048]{1,0:T(8,128)(2,1)} %k_ref.1, bf16[128,2048]{1,0:T(8,128)(2,1)} %v_ref.1, bf16[128,2048]{1,0:T(8,128)(2,1)} %g_ref.1), custom_call_target="tpu_custom_call" | custom-call | tf_op jit(solution)/shard_map/pallas_call | solution.py:359
  113.7 0.0 copy-start.1
  113.7 1.9 %copy.12 = bf16[128,2048]{1,0:T(8,128)(2,1)} copy(bf16[128,2048]{1,0:T(8,128)(2,1)} %get-tuple-element.6) | data formatting | bytes 1048576
  115.6 0.0 copy-done.1
  115.6 0.0 copy-start
  115.6 0.8 copy.13
  116.4 0.4 copy-done
  116.9 0.8 copy.14
Async XLA Ops:
  113.7 2.0 %copy-start.1 = (bf16[128,2048]{1,0:T(8,128)(2,1)S(1)}, bf16[128,2048]{1,0:T(8,128)(2,1)}, u32[]{:S(2)}) copy-start(bf16[128,2048]{1,0:T(8,128)(2,1)} %get-tuple-element.7) | copy-start | bytes 1572868
  115.6 1.2 %copy-start = (bf16[128,2048]{1,0:T(8,128)(2,1)S(1)}, bf16[128,2048]{1,0:T(8,128)(2,1)}, u32[]{:S(2)}) copy-start(bf16[128,2048]{1,0:T(8,128)(2,1)} %get-tuple-element.8) | copy-start | bytes 1572868

commit v3 on v2

--- a/solution.py
+++ b/solution.py
@@ -77,14 +77,16 @@
             fin.at[c, i, other_rows, :], outs[i].at[:, cols(x, c)], osend.at[c, i],
             orecv.at[c, i], device_id=partner, device_id_type=MESH)
 
-    def forward(c, src, dst, sem, to):
-        return pltpu.make_async_remote_copy(
-            qg.at[src, c], qg.at[dst, c], fsend.at[c, sem], frecv.at[c, dst - 1],
+    def forward(c, src, dst, sem, to, rows=None):
+        rows = pl.ds(0, rows or size)
+        return pltpu.make_async_remote_copy(
+            qg.at[src, c, :, rows, :], qg.at[dst, c, :, rows, :], fsend.at[c, sem], frecv.at[c, dst - 1],
             device_id=to, device_id_type=MESH)
 
-    def back(c, d, dst, to):
-        return pltpu.make_async_remote_copy(
-            rout.at[d - 1, c], slot.at[dst, c], rsend.at[c, d - 1], rrecv.at[c, dst],
+    def back(c, d, dst, to, rows=None):
+        rows = pl.ds(0, rows or size)
+        return pltpu.make_async_remote_copy(
+            rout.at[d - 1, c, rows, :], slot.at[dst, c, rows, :], rsend.at[c, d - 1], rrecv.at[c, dst],
             device_id=to, device_id_type=MESH)
 
     def partial(c, d):
@@ -97,11 +99,11 @@
             whole_out.at[c], whole_in.at[c, d], tsend.at[c, d - 1], trecv.at[c, d - 1],
             device_id=dev(-d, x), device_id_type=MESH)
 
-    def arrived(c, d):
-        forward(c, 0, d, 0, up).wait_recv()
-
-    def returned(c, dst):
-        back(c, 1, dst, up).wait_recv()
+    def arrived(c, d, rows=None):
+        forward(c, 0, d, 0, up, rows).wait_recv()
+
+    def returned(c, dst, rows=None):
+        back(c, 1, dst, up, rows).wait_recv()
 
     def every_chunk(body):
         def step(c, carry):
@@ -136,9 +138,13 @@
         def _():
             forward(c, 0, 1, 0, up).start()
 
-        @when(low)
+        @when(z >= 2)
         def _():
             forward(c, 0, 3, 1, ahead).start()
+
+        @when(z == 1)
+        def _():
+            forward(c, 0, 3, 1, ahead, tok).start()
 
     def stage_b1(c):
         @when(low)
@@ -149,20 +155,21 @@
             def _():
                 forward(c, 1, 2, 2, up).start()
 
-        @when(high)
+        @when(z == 0)
+        def _():
+            arrived(c, 3, tok)
+
+        @when(low, high)
         def _():
             arrived(c, 3)
-
-            @when(low)
-            def _():
-                forward(c, 3, 2, 3, down).start()
+            forward(c, 3, 2, 3, down).start()
 
     def stage_b2(c):
         arrived(c, 2)
 
         @when(z == 2)
         def _():
-            forward(c, 2, 3, 4, up).start()
+            forward(c, 2, 3, 4, up, tok).start()
 
         @when(z == 1)
         def _():
@@ -175,7 +182,7 @@
 
         @when(z == LINE - 1)
         def _():
-            arrived(c, 3)
+            arrived(c, 3, tok)
 
         @when(z == 0)
         def _():
@@ -245,7 +252,7 @@
         @when(z == LINE - 1)
         def _():
             rout[2, c] = acc[c, 3].astype(jnp.bfloat16)
-            back(c, 3, 2, down).start()
+            back(c, 3, 2, down, tok).start()
 
         @when(z == 0)
         def _():
@@ -256,37 +263,56 @@
             local_out(i, c).start()
             cross_out(i, c).start()
 
-    def fold(c, d, has_child, source):
-        @when(has_child)
-        def _():
-            returned(c, source)
-            rout[d - 1, c] = (acc[c, d] + slot[source, c].astype(jnp.float32)).astype(jnp.bfloat16)
-
-        @when(jnp.logical_not(has_child))
-        def _():
-            rout[d - 1, c] = acc[c, d].astype(jnp.bfloat16)
+    def fold(c, d, source, rows=None):
+        rows = rows or size
+        returned(c, source, rows)
+        rout[d - 1, c, :rows] = (
+            acc[c, d, :rows] + slot[source, c, :rows].astype(jnp.float32)
+        ).astype(jnp.bfloat16)
+        if rows < size:
+            rout[d - 1, c, rows:] = acc[c, d, rows:].astype(jnp.bfloat16)
+
+    def plain(c, d):
+        rout[d - 1, c] = acc[c, d].astype(jnp.bfloat16)
 
     def stage_r2(c):
-        fold(c, 2, jnp.logical_and(low, high), 2)
-
-        @when(z >= 2)
-        def _():
+        @when(z == 0)
+        def _():
+            plain(c, 2)
+            back(c, 2, 3, up).start()
+
+        @when(z == 1)
+        def _():
+            fold(c, 2, 2)
+            back(c, 2, 3, up).start()
+
+        @when(z == 2)
+        def _():
+            fold(c, 2, 2, tok)
             back(c, 2, 1, down).start()
 
-        @when(z < 2)
-        def _():
-            back(c, 2, 3, up).start()
+        @when(z == 3)
+        def _():
+            plain(c, 2)
+            back(c, 2, 1, down).start()
 
     def stage_r1(c):
-        @when(low)
-        def _():
-            fold(c, 1, high, 1)
+        @when(z == LINE - 1)
+        def _():
+            plain(c, 1)
             back(c, 1, 0, down).start()
 
-        @when(high)
-        def _():
-            fold(c, 3, low, 3)
+        @when(low, high)
+        def _():
+            fold(c, 1, 1)
+            back(c, 1, 0, down).start()
+            fold(c, 3, 3)
             back(c, 3, 4, behind).start()
+
+        @when(z == 0)
+        def _():
+            plain(c, 3)
+            back(c, 3, 4, behind, tok).start()
 
     def stage_r0(c):
         @when(high)
@@ -294,10 +320,15 @@
             returned(c, 0)
             acc[c, 0] = acc[c, 0] + slot[0, c].astype(jnp.float32)
 
-        @when(low)
+        @when(z >= 2)
         def _():
             returned(c, 4)
             acc[c, 0] = acc[c, 0] + slot[4, c].astype(jnp.float32)
+
+        @when(z == 1)
+        def _():
+            returned(c, 4, tok)
+            acc[c, 0, :tok] = acc[c, 0, :tok] + slot[4, c, :tok].astype(jnp.float32)
 
         fin[c, 0] = acc[c, 0].astype(jnp.bfloat16)
         local_out(0, c).start()
@@ -330,17 +361,31 @@
         def _():
             forward(c, 0, 1, 0, up).wait_send()
 
-        @when(low)
+        @when(z >= 2)
         def _():
             forward(c, 0, 3, 1, ahead).wait_send()
+
+        @when(z == 1)
+        def _():
+            forward(c, 0, 3, 1, ahead, tok).wait_send()
+            forward(c, 2, 1, 4, down).wait_send()
+
+        @when(z == 2)
+        def _():
+            forward(c, 2, 3, 4, up, tok).wait_send()
 
         @when(low, high)
         def _():
             forward(c, 1, 2, 2, up).wait_send()
             forward(c, 3, 2, 3, down).wait_send()
-            forward(c, 2, 3, 4, up).wait_send()
+            back(c, 3, 0, up).wait_send()
+
+        @when(jnp.logical_not(jnp.logical_and(low, high)))
+        def _():
+            back(c, 3, 0, up, tok).wait_send()
         for d in range(1, 4):
-            back(c, d, 0, up).wait_send()
+            if d < 3:
+                back(c, d, 0, up).wait_send()
             partial(c, d).wait_send()
             totals(c, d).wait_send()
 

time: 118 us -> 107 us (0.907)
  Pallas kernels: 112 us -> 102 us
    pallas_call x1, Pallas kernels: 112 us -> 102 us  [per_device(): pl.pallas_call(functools.partial(kernel, (outer, inner, tok, heads)), out...]
where the time goes in v3:
time: 107 us
  Pallas kernels  102 us (95%)
  local copies, waits for them, and re-layouts  3.97 us (4%)
  between operations  1.3 us (1%)
    pallas_call x1, Pallas kernels, per_device(): pl.pallas_call(functools.partial(kernel, (outer, inner, tok, heads)), out...  102 us
    unnamed x7, local copies, waits for them, and re-layouts  3.97 us

profile of v3, /device:TPU:0, one launch (start us, length us, event | category | flops | bytes accessed | tf_op | source)
XLA Modules:
  0.0 107.1 jit_solution(681770058031718809)
XLA Ops:
  1.3 101.8 %shard_map.76 = (bf16[128,2048]{1,0:T(8,128)(2,1)}, bf16[128,2048]{1,0:T(8,128)(2,1)}, bf16[128,2048]{1,0:T(8,128)(2,1)}) custom-call(s32[1]{0:T(128)S(6)} %copy.11.window, bf16[128,2048]{1,0:T(8,128)(2,1)} %q_ref.1, bf16[128,2048]{1,0:T(8,128)(2,1)} %k_ref.1, bf16[128,2048]{1,0:T(8,128)(2,1)} %v_ref.1, bf16[128,2048]{1,0:T(8,128)(2,1)} %g_ref.1), custom_call_target="tpu_custom_call" | custom-call | tf_op jit(solution)/shard_map/pallas_call | solution.py:404
  103.1 0.0 copy-start.1
  103.1 1.9 %copy.12 = bf16[128,2048]{1,0:T(8,128)(2,1)} copy(bf16[128,2048]{1,0:T(8,128)(2,1)} %get-tuple-element.6) | data formatting | bytes 1048576
  105.1 0.0 copy-done.1
  105.1 0.0 copy-start
  105.1 0.8 copy.13
  105.9 0.4 copy-done
  106.3 0.8 copy.14
Async XLA Ops:
  103.1 2.0 %copy-start.1 = (bf16[128,2048]{1,0:T(8,128)(2,1)S(1)}, bf16[128,2048]{1,0:T(8,128)(2,1)}, u32[]{:S(2)}) copy-start(bf16[128,2048]{1,0:T(8,128)(2,1)} %get-tuple-element.7) | copy-start | bytes 1572868
  105.1 1.2 %copy-start = (bf16[128,2048]{1,0:T(8,128)(2,1)S(1)}, bf16[128,2048]{1,0:T(8,128)(2,1)}, u32[]{:S(2)}) copy-start(bf16[128,2048]{1,0:T(8,128)(2,1)} %get-tuple-element.8) | copy-start | bytes 1572868

commit v4 on v3

--- a/solution.py
+++ b/solution.py
@@ -334,12 +334,20 @@
         local_out(0, c).start()
         cross_out(0, c).start()
 
-    stages = (
-        stage_a, stage_b1, stage_b2, stage_c, stage_s1, stage_s2, stage_r2, stage_r1, stage_r0
+    schedule = (
+        (stage_a, 0),
+        (stage_b1, 1),
+        (stage_b2, 2),
+        (stage_c, 3),
+        (stage_s1, 4),
+        (stage_s2, 5),
+        (stage_r2, 6),
+        (stage_r1, 7),
+        (stage_r0, 8),
     )
 
     def tick(t, carry):
-        for lag, stage in enumerate(stages):
+        for stage, lag in schedule:
             c = t - lag
 
             @when(c >= 0, c < chunks)
@@ -347,7 +355,7 @@
                 stage(c)
         return carry
 
-    lax.fori_loop(0, chunks + len(stages) - 1, tick, 0)
+    lax.fori_loop(0, chunks + max(lag for _, lag in schedule), tick, 0)
 
     @every_chunk
     def _(c):
@@ -397,15 +405,14 @@
     chunks = heads // 2
     size = 2 * tok
     low, full = jnp.bfloat16, jnp.float32
-    vmem = pl.BlockSpec(memory_space=pltpu.VMEM)
     block = (chunks, 2, size, HD)
     sums = (chunks, size, HD)
     sems = (4, 4, 4, 5, 3, 3, 5, 3, 3, 3, 3, 3, 3, 3)
     return pl.pallas_call(
         functools.partial(kernel, (outer, inner, tok, heads)),
         out_shape=[jax.ShapeDtypeStruct((tok, columns), low)] * 3,
-        in_specs=[pl.BlockSpec(memory_space=pltpu.SMEM)] + [vmem] * 4,
-        out_specs=[vmem] * 3,
+        in_specs=[pl.BlockSpec(memory_space=pltpu.SMEM)] + [pl.BlockSpec(memory_space=pl.ANY)] * 4,
+        out_specs=[pl.BlockSpec(memory_space=pl.ANY)] * 3,
         scratch_shapes=[
             pltpu.VMEM((4,) + block, low),
             pltpu.VMEM(block, low),

time: 107 us -> 104 us (0.972)
  Pallas kernels: 102 us -> 99 us
    pallas_call x1, Pallas kernels: 102 us -> 99 us  [per_device(): pl.pallas_call(functools.partial(kernel, (outer, inner, tok, heads)), out...]
where the time goes in v4:
time: 104 us
  Pallas kernels  99 us (95%)
  local copies, waits for them, and re-layouts  3.97 us (4%)
  between operations  1.3 us (1%)
    pallas_call x1, Pallas kernels, per_device(): pl.pallas_call(functools.partial(kernel, (outer, inner, tok, heads)), out...  99 us
    unnamed x7, local copies, waits for them, and re-layouts  3.97 us

profile of v4, /device:TPU:0, one launch (start us, length us, event | category | flops | bytes accessed | tf_op | source)
XLA Modules:
  0.0 104.3 jit_solution(13416790219034189763)
XLA Ops:
  1.3 99.0 %shard_map.76 = (bf16[128,2048]{1,0:T(8,128)(2,1)}, bf16[128,2048]{1,0:T(8,128)(2,1)}, bf16[128,2048]{1,0:T(8,128)(2,1)}) custom-call(s32[1]{0:T(128)S(6)} %copy.11.window, bf16[128,2048]{1,0:T(8,128)(2,1)} %q_ref.1, bf16[128,2048]{1,0:T(8,128)(2,1)} %k_ref.1, bf16[128,2048]{1,0:T(8,128)(2,1)} %v_ref.1, bf16[128,2048]{1,0:T(8,128)(2,1)} %g_ref.1), custom_call_target="tpu_custom_call" | custom-call | tf_op jit(solution)/shard_map/pallas_call | solution.py:411
  100.3 0.0 copy-start.1
  100.3 1.9 %copy.12 = bf16[128,2048]{1,0:T(8,128)(2,1)} copy(bf16[128,2048]{1,0:T(8,128)(2,1)} %get-tuple-element.6) | data formatting | bytes 1048576
  102.3 0.0 copy-done.1
  102.3 0.0 copy-start
  102.3 0.8 copy.13
  103.1 0.4 copy-done
  103.5 0.8 copy.14
Async XLA Ops:
  100.3 2.0 %copy-start.1 = (bf16[128,2048]{1,0:T(8,128)(2,1)S(1)}, bf16[128,2048]{1,0:T(8,128)(2,1)}, u32[]{:S(2)}) copy-start(bf16[128,2048]{1,0:T(8,128)(2,1)} %get-tuple-element.7) | copy-start | bytes 1572868
  102.3 1.2 %copy-start = (bf16[128,2048]{1,0:T(8,128)(2,1)S(1)}, bf16[128,2048]{1,0:T(8,128)(2,1)}, u32[]{:S(2)}) copy-start(bf16[128,2048]{1,0:T(8,128)(2,1)} %get-tuple-element.8) | copy-start | bytes 1572868
